TPU v7x, 128 devices: a whole 4x4x4 slice. The times are simulated.
128 devices in a mesh: req: 16 (over y, x), seq: 8 (over z, core).
Axes of the slice: x: 4, y: 4, z: 4, core: 2. Of those that a mesh axis runs over, the one named last changes fastest.
Arguments:
- qkv_proj: bfloat16 [16, 1024, 4096], P('req', 'seq'), may hold values from -6 to 6
- gate_proj: bfloat16 [16, 1024, 2048], P('req', 'seq'), may hold values from -6 to 6
- residual: bfloat16 [16, 1024, 2048], P('req', 'seq'), may hold values from -6 to 6
- log_decay: float32 [16, 1024, 8], P('req', 'seq'), may hold values from -1 to 0, as said below
- beta_logit: bfloat16 [16, 1024, 8], P('req', 'seq'), may hold values from -6 to 6
- lengths: int32 [16], replicated, may hold values from 1 to 1024, 8192 in all
- slot_request: int32 [16], replicated, may hold values from 0 to 15, each once
- conv_weight: float32 [4, 4096], replicated, may hold values from -3 to 3
- norm_gain: float32 [256], replicated, may hold values from 0.1 to 1.9
- out_weight: bfloat16 [2048, 2048], P(('req', 'seq')), may hold values from -0.125 to 0.125
- mlp_gain: float32 [2048], replicated, may hold values from 0.1 to 1.9
- w_gate: bfloat16 [2048, 5632], P('req', 'seq'), may hold values from -0.125 to 0.125
- w_up: bfloat16 [2048, 5632], P('req', 'seq'), may hold values from -0.125 to 0.125
- w_down: bfloat16 [5632, 2048], P('seq', 'req'), may hold values from -0.078125 to 0.078125
Outputs:
- hidden_out: bfloat16 [16, 1024, 2048], P('req', 'seq')
- final_state: float32 [16, 8, 128, 256], P('req', 'seq')
- conv_edge: bfloat16 [16, 3, 4096], P('req', None, 'seq')
Inputs may be any that keep to these rules, and one draw needn't show every extreme that they name: Slot s of the req axis holds request slot_request[s]. The 16 lengths sum to 8192, and the longest is exactly 1024. `log_decay`: every entry is negative.
All inputs are finite; a program needn't handle non-finite values.
Results may differ from a plain program's by a relative error of at most 0.014.
Values may be sent and summed in bfloat16 or wider, within the bound.
A program may use at most 128 MiB of HBM per device.

v0:
```python
import jax
import jax.numpy as jnp
from jax import lax
from jax.sharding import PartitionSpec as P

LOCAL_HEADS = 8
DK = 128
DV = 256
CONV = 4
BLOCK = 64
HK = 1024
EPS_NORM = 1e-05
EPS_UNIT = 1e-06
HIGHEST = lax.Precision.HIGHEST


def shifted(value, axis, steps):
    count = lax.axis_size(axis)
    initial, last = (max(0, -steps), min(count, count - steps))
    return lax.ppermute(value, axis, [(source, source + steps) for source in range(initial, last)])


def unit_norm(vector):
    return vector * lax.rsqrt(jnp.sum(vector * vector, axis=-1, keepdims=True) + EPS_UNIT)


def to_blocks(tensor, block_len):
    length = tensor.shape[0]
    grouped = tensor.reshape((length // block_len, block_len) + tensor.shape[1:])
    return jnp.moveaxis(grouped, 2, 0)


def block_tables(query_vec, key_vecs, beta_gate, decay_log, block_len):
    query_b = to_blocks(query_vec, block_len)
    keys_b = to_blocks(key_vecs, block_len)
    beta_b = to_blocks(beta_gate, block_len)
    cumulative = jnp.cumsum(to_blocks(decay_log, block_len), axis=-1)
    spread = cumulative[..., :, None] - cumulative[..., None, :]
    lower_full = jnp.tril(jnp.ones((block_len, block_len), jnp.float32))
    lower_strict = jnp.tril(jnp.ones((block_len, block_len), jnp.float32), -1)
    within = jnp.exp(jnp.where(lower_full > 0, spread, 0.0)) * lower_full
    key_inner = jnp.einsum("hnik,hnjk->hnij", keys_b, keys_b, precision=HIGHEST)
    couple = beta_b[..., :, None] * within * lower_strict * key_inner
    identity = jnp.broadcast_to(jnp.eye(block_len, dtype=jnp.float32), couple.shape)
    inverse = lax.linalg.triangular_solve(
        identity + couple, identity, left_side=True, lower=True, unit_diagonal=True
    )
    growth = jnp.exp(cumulative)
    weighted_keys = jnp.einsum(
        "hnij,hnjk->hnik", inverse, (beta_b * growth)[..., None] * keys_b, precision=HIGHEST
    )
    query_keys = jnp.einsum("hnik,hnjk->hnij", query_b, keys_b, precision=HIGHEST) * within
    grown_query = growth[..., None] * query_b
    keys_to_end = jnp.exp(cumulative[..., -1:] - cumulative)[..., None] * keys_b
    end_growth = growth[..., -1]
    return (inverse, beta_b, (weighted_keys, query_keys, grown_query, keys_to_end, end_growth))


def solve_values(inverse, beta_b, values_b):
    return jnp.einsum("hnij,hnjx->hnix", inverse, beta_b[..., None] * values_b, precision=HIGHEST)


def run_blocks(initial, solved, tables):
    weighted_keys, query_keys, grown_query, keys_to_end, end_growth = tables
    sequence = tuple(
        (
            jnp.moveaxis(tensor, 1, 0)
            for tensor in (solved, weighted_keys, query_keys, grown_query, keys_to_end, end_growth)
        )
    )

    def advance(running, inputs_now):
        solved_now, weighted_now, inner_now, query_now, keys_now, growth_now = inputs_now
        corrected = solved_now - jnp.einsum(
            "hck,hkx->hcx", weighted_now, running, precision=HIGHEST
        )
        output_now = jnp.einsum("hck,hkx->hcx", query_now, running, precision=HIGHEST) + jnp.einsum(
            "hcd,hdx->hcx", inner_now, corrected, precision=HIGHEST
        )
        running = growth_now[:, None, None] * running + jnp.einsum(
            "hck,hcx->hkx", keys_now, corrected, precision=HIGHEST
        )
        return (running, output_now)

    return lax.scan(advance, initial, sequence)


def local(
    qkv_proj,
    gate_proj,
    residual,
    log_decay,
    beta_logit,
    lengths,
    slot_request,
    conv_weight,
    norm_gain,
    out_weight,
    mlp_gain,
    w_gate,
    w_up,
    w_down,
):
    seq_index = lax.axis_index("seq")
    req_index = lax.axis_index("req")
    seq_size = lax.axis_size("seq")
    piece_len = qkv_proj.shape[1]
    channels = qkv_proj.shape[2]
    request_ids = jnp.arange(slot_request.shape[0], dtype=jnp.int32)
    request = jnp.sum(jnp.where(request_ids == req_index, slot_request, 0))
    length = jnp.sum(jnp.where(request_ids == request, lengths, 0))
    position = seq_index * piece_len + jnp.arange(piece_len, dtype=jnp.int32)
    live_mask = position < length
    tokens = qkv_proj[0]
    rim_rows = shifted(tokens[piece_len - (CONV - 1) :], "seq", 1)
    extended = jnp.concatenate([rim_rows, tokens], axis=0)
    convolved = jnp.zeros((piece_len, channels), jnp.float32)
    for offset in range(CONV):
        convolved = convolved + conv_weight[offset] * extended[offset : offset + piece_len].astype(
            jnp.float32
        )
    activated = jax.nn.silu(convolved)
    query_vec = unit_norm(activated[:, :HK].reshape(piece_len, LOCAL_HEADS, DK)) * DK ** (-0.5)
    key_vecs = unit_norm(activated[:, HK : 2 * HK].reshape(piece_len, LOCAL_HEADS, DK))
    values = activated[:, 2 * HK :].reshape(piece_len, LOCAL_HEADS, DV)
    beta_gate = jax.nn.sigmoid(beta_logit[0].astype(jnp.float32)) * live_mask[:, None]
    decay_log = jnp.where(live_mask[:, None], log_decay[0], 0.0)
    inverse, beta_b, tables = block_tables(query_vec, key_vecs, beta_gate, decay_log, BLOCK)
    values_b = to_blocks(values, BLOCK)
    solved = solve_values(inverse, beta_b, values_b)
    zero_state = jnp.zeros((LOCAL_HEADS, DK, DV), jnp.float32)
    incoming = zero_state
    for section_index in range(seq_size - 1):
        ending, discarded = run_blocks(incoming, solved, tables)
        incoming = shifted(ending.astype(jnp.bfloat16), "seq", 1).astype(ending.dtype)
    ending, outputs = run_blocks(incoming, solved, tables)
    outputs = jnp.moveaxis(outputs, 1, 2).reshape(piece_len, LOCAL_HEADS, DV)
    is_last = seq_index == seq_size - 1
    state_term = jnp.where(is_last, ending, 0.0)
    targets = length - (CONV - 1) + jnp.arange(CONV - 1, dtype=jnp.int32)
    select = (position[None, :] == targets[:, None]).astype(jnp.bfloat16)
    edge_term = jnp.dot(select, tokens, preferred_element_type=jnp.float32)
    state_part, edge_part = (
        lax.psum_scatter(
            state_term.astype(jnp.bfloat16), "seq", scatter_dimension=0, tiled=True
        ).astype(jnp.float32),
        lax.psum_scatter(
            edge_term.astype(jnp.bfloat16), "seq", scatter_dimension=1, tiled=True
        ).astype(jnp.float32),
    )
    gate_values = gate_proj[0].astype(jnp.float32).reshape(piece_len, LOCAL_HEADS, DV)
    scaled = outputs * lax.rsqrt(jnp.mean(outputs * outputs, axis=-1, keepdims=True) + EPS_NORM)
    mixed_heads = (
        (scaled * norm_gain * jax.nn.silu(gate_values))
        .reshape(piece_len, LOCAL_HEADS * DV)
        .astype(jnp.bfloat16)
    )
    attended = jnp.dot(
        mixed_heads,
        lax.all_gather(out_weight, ("req", "seq"), axis=0, tiled=True),
        preferred_element_type=jnp.float32,
    )
    hidden_state = (residual[0].astype(jnp.float32) + attended).astype(jnp.bfloat16)
    stream = hidden_state.astype(jnp.float32)
    normed = (
        stream * lax.rsqrt(jnp.mean(stream * stream, axis=-1, keepdims=True) + EPS_NORM) * mlp_gain
    ).astype(jnp.bfloat16)
    gate_full, up_full = (
        lax.all_gather(w_gate, "req", axis=0, tiled=True),
        lax.all_gather(w_up, "req", axis=0, tiled=True),
    )
    down_full = lax.all_gather(w_down, "req", axis=1, tiled=True)
    shard_rows = lax.all_gather(normed, "seq", axis=0, tiled=True)
    gate_part = jnp.dot(shard_rows, gate_full, preferred_element_type=jnp.float32)
    upward = jnp.dot(shard_rows, up_full, preferred_element_type=jnp.float32)
    inner_units = (jax.nn.silu(gate_part) * upward).astype(jnp.bfloat16)
    summed = lax.psum_scatter(
        jnp.dot(inner_units, down_full, preferred_element_type=jnp.float32).astype(jnp.bfloat16),
        "seq",
        scatter_dimension=0,
        tiled=True,
    ).astype(jnp.float32)
    combined = stream + summed
    hidden_out = jnp.where(live_mask[:, None], combined, 0.0).astype(jnp.bfloat16)
    return (hidden_out[None], state_part[None], edge_part.astype(jnp.bfloat16)[None])


def solution(mesh):
    return jax.shard_map(
        local,
        mesh=mesh,
        in_specs=(
            P("req", "seq", None),
            P("req", "seq", None),
            P("req", "seq", None),
            P("req", "seq", None),
            P("req", "seq", None),
            P(),
            P(),
            P(),
            P(),
            P(("req", "seq"), None),
            P(),
            P("req", "seq"),
            P("req", "seq"),
            P("seq", "req"),
        ),
        out_specs=(P("req", "seq", None), P("req", "seq", None, None), P("req", None, "seq")),
        check_vma=False,
    )
```

profile of v0, /device:TPU:0, one launch (start us, length us, event | category | flops | bytes accessed | tf_op | source)
XLA Modules:
  0.0 511.9 jit_solution(8159952312244182873)
XLA Ops:
  8.1 1.3 collective-permute-start
  11.0 1.3 fusion.105
  12.3 1.9 fusion.106
  17.2 3.4 divide_multiply_fusion
  20.6 1.4 multiply_bitcast_fusion
  22.8 1.1 broadcast_multiply_fusion
  23.9 1.8 fusion.72
  25.7 80.0 %custom-call.3 = f32[8,2,1,64,64]{3,4,2,1,0:T(8,128)} custom-call(f32[8,2,1,64,64]{4,3,2,1,0:T(8,128)} %fusion.72), custom_call_target="InvertDiagBlocksLowerTriangular" | custom-call | tf_op jit(solution)/shard_map/triangular_solve | solution.py:45
  105.7 2.0 fusion.85
  107.8 1.7 convolution_bitcast_fusion.2
  109.9 1.3 convolution_bitcast_fusion
  111.8 4.1 while.90
  112.5 1.3 convolution_add_fusion.25
  114.6 1.3 convolution_add_fusion.25
  116.8 5.9 %collective-permute-start.1 = (bf16[8,128,256]{2,1,0:T(8,128)(2,1)}, bf16[8,128,256]{2,1,0:T(8,128)(2,1)}, u32[]{:S(2)}, u32[]{:S(2)}) collective-permute-start(bf16[8,128,256]{2,1,0:T(8,128)(2,1)} %convert_element_type.129), channel_id=1, source_target_pairs={{0,1},{1,2},{2,3},{3,4},{4,5},{5,6},{6,7},{8,9},{9,10},{10,11},{11... | collective-permute-start | bytes 1572872 | tf_op jit(solution)/shard_map/ppermute | solution.py:20
  124.5 4.2 while.83
  125.3 1.3 convolution_add_fusion.18
  127.4 1.3 convolution_add_fusion.18
  129.6 7.3 %collective-permute-start.2 = (bf16[8,128,256]{2,1,0:T(8,128)(2,1)}, bf16[8,128,256]{2,1,0:T(8,128)(2,1)}, u32[]{:S(2)}, u32[]{:S(2)}) collective-permute-start(bf16[8,128,256]{2,1,0:T(8,128)(2,1)} %convert_element_type.131), channel_id=1, source_target_pairs={{0,1},{1,2},{2,3},{3,4},{4,5},{5,6},{6,7},{8,9},{9,10},{10,11},{11... | collective-permute-start | bytes 1572872 | tf_op jit(solution)/shard_map/ppermute | solution.py:20
  139.1 4.2 while.84
  139.8 1.3 convolution_add_fusion.19
  141.9 1.3 convolution_add_fusion.19
  144.2 9.7 %collective-permute-start.3 = (bf16[8,128,256]{2,1,0:T(8,128)(2,1)}, bf16[8,128,256]{2,1,0:T(8,128)(2,1)}, u32[]{:S(2)}, u32[]{:S(2)}) collective-permute-start(bf16[8,128,256]{2,1,0:T(8,128)(2,1)} %convert_element_type.133), channel_id=1, source_target_pairs={{0,1},{1,2},{2,3},{3,4},{4,5},{5,6},{6,7},{8,9},{9,10},{10,11},{11... | collective-permute-start | bytes 1572872 | tf_op jit(solution)/shard_map/ppermute | solution.py:20
  156.1 4.2 while.85
  156.9 1.3 convolution_add_fusion.20
  159.0 1.3 convolution_add_fusion.20
  161.2 9.7 %collective-permute-start.4 = (bf16[8,128,256]{2,1,0:T(8,128)(2,1)}, bf16[8,128,256]{2,1,0:T(8,128)(2,1)}, u32[]{:S(2)}, u32[]{:S(2)}) collective-permute-start(bf16[8,128,256]{2,1,0:T(8,128)(2,1)} %convert_element_type.135), channel_id=1, source_target_pairs={{0,1},{1,2},{2,3},{3,4},{4,5},{5,6},{6,7},{8,9},{9,10},{10,11},{11... | collective-permute-start | bytes 1572872 | tf_op jit(solution)/shard_map/ppermute | solution.py:20
  173.2 4.2 while.86
  173.9 1.3 convolution_add_fusion.21
  176.0 1.3 convolution_add_fusion.21
  178.3 9.7 %collective-permute-start.5 = (bf16[8,128,256]{2,1,0:T(8,128)(2,1)}, bf16[8,128,256]{2,1,0:T(8,128)(2,1)}, u32[]{:S(2)}, u32[]{:S(2)}) collective-permute-start(bf16[8,128,256]{2,1,0:T(8,128)(2,1)} %convert_element_type.137), channel_id=1, source_target_pairs={{0,1},{1,2},{2,3},{3,4},{4,5},{5,6},{6,7},{8,9},{9,10},{10,11},{11... | collective-permute-start | bytes 1572872 | tf_op jit(solution)/shard_map/ppermute | solution.py:20
  190.2 4.2 while.87
  191.0 1.3 convolution_add_fusion.22
  193.0 1.3 convolution_add_fusion.22
  195.2 9.7 %collective-permute-start.6 = (bf16[8,128,256]{2,1,0:T(8,128)(2,1)}, bf16[8,128,256]{2,1,0:T(8,128)(2,1)}, u32[]{:S(2)}, u32[]{:S(2)}) collective-permute-start(bf16[8,128,256]{2,1,0:T(8,128)(2,1)} %convert_element_type.139), channel_id=1, source_target_pairs={{0,1},{1,2},{2,3},{3,4},{4,5},{5,6},{6,7},{8,9},{9,10},{10,11},{11... | collective-permute-start | bytes 1572872 | tf_op jit(solution)/shard_map/ppermute | solution.py:20
  206.9 1.9 copy.258
  210.0 4.2 while.88
  210.7 1.3 convolution_add_fusion.23
  212.8 1.3 convolution_add_fusion.23
  214.2 6.3 %collective-permute-start.7 = (bf16[8,128,256]{2,1,0:T(8,128)(2,1)S(1)}, bf16[8,128,256]{2,1,0:T(8,128)(2,1)S(1)}, u32[]{:S(2)}, u32[]{:S(2)}) collective-permute-start(bf16[8,128,256]{2,1,0:T(8,128)(2,1)S(1)} %convert_element_type.141), channel_id=1, source_target_pairs={{0,1},{1,2},{2,3},{3,4},{4,5},{5,6},{6,7},{8,9},{9,10},{10,11},{11... | collective-permute-start | bytes 1572872 | tf_op jit(solution)/shard_map/ppermute | solution.py:20
  220.5 1.2 fusion.95
  222.9 1.9 fusion.70
  224.9 10.8 %while.89 = (s32[]{:T(128)}, f32[8,128,256]{2,1,0:T(8,128)S(1)}, f32[2,8,64,256]{3,2,1,0:T(8,128)}, f32[2,8]{1,0:T(2,128)S(1)}, f32[2,8,64,128]{3,2,1,0:T(8,128)...) while((s32[]{:T(128)}, f32[8,128,256]{2,1,0:T(8,128)S(1)}, ...), condition=%wide.region_20.21_spmd, body=%wide.region_19.20_spmd.sunk | while | flops 705429504 | bytes 19925256 | solution.py:85
  225.7 1.5 fusion.223
  229.0 1.3 convolution_add_fusion.24
  231.1 1.5 fusion.223
  234.4 1.3 convolution_add_fusion.24
  235.8 1.5 multiply_reduce_fusion.1
  237.6 1.4 copy.261
  239.6 1.3 copy.260
  241.0 5.8 %multiply_reduce_fusion = (f32[128]{0:T(128)S(1)}, f32[128,2048]{1,0:T(8,128)S(1)}) fusion(bf16[2048,2048]{1,0:T(8,128)(2,1)} %all-gather.6.cloned.1.call-done, f32[128,2048]{1,0:T(8,128)} %bitcast.348, f32[128,2048]{1,0:T(8,128)} %bitcast.347, bf16[1,128,2048]{2,1,0:T(8,128)(2,1)} %param.31, f32[2048]{0:T(1024)S(1)} %bitcast.360, ...), kind=kOutput, calls=%fused_computation.125 | convolution fusion | flops 1077673856 | bytes 12591616 | tf_op jit(solution)/shard_map/dot_general | solution.py:158
  249.9 1.4 copy.250
  252.6 6.2 %all-gather.10.cloned.1.call-done = bf16[2048,704]{0,1:T(8,128)(2,1)} async-done(((bf16[128,704]{0,1:T(8,128)(2,1)}), bf16[2048,704]{0,1:T(8,128)(2,1)}) %all-gather.10.cloned.1.call-update) | async-done | bytes 2883600 | tf_op jit(solution)/shard_map/all_gather | solution.py:169
  258.8 34.0 %all-gather.8.cloned.1.call-done = bf16[1024,2048]{1,0:T(8,128)(2,1)} async-done(((bf16[128,2048]{1,0:T(8,128)(2,1)}), bf16[1024,2048]{1,0:T(8,128)(2,1)}) %all-gather.8.cloned.1.call-update) | async-done | bytes 4194320 | tf_op jit(solution)/shard_map/all_gather | solution.py:173
  292.8 7.8 %fusion.114 = f32[1024,704]{0,1:T(8,128)} fusion(bf16[1024,2048]{1,0:T(8,128)(2,1)} %all-gather.8.cloned.1.call-done, bf16[2048,704]{0,1:T(8,128)(2,1)} %all-gather.10.cloned.1.call-done), kind=kOutput, calls=%fused_computation.195 | convolution fusion | flops 2952790016 | bytes 9961472 | tf_op jit(solution)/shard_map/dot_general | solution.py:174
  300.7 44.4 %all-gather.12.cloned.1.call-done = bf16[2048,704]{0,1:T(8,128)(2,1)} async-done(((bf16[128,704]{0,1:T(8,128)(2,1)}), bf16[2048,704]{0,1:T(8,128)(2,1)}) %all-gather.12.cloned.1.call-update) | async-done | bytes 2883600 | tf_op jit(solution)/shard_map/all_gather | solution.py:170
  345.1 51.8 %all-gather.14.cloned.1.call-done = bf16[704,2048]{1,0:T(8,128)(2,1)} async-done(((bf16[704,128]{1,0:T(8,128)(2,1)}), bf16[704,2048]{1,0:T(8,128)(2,1)}) %all-gather.14.cloned.1.call-update) | async-done | bytes 2883600 | tf_op jit(solution)/shard_map/all_gather | solution.py:172
  396.9 12.0 %convolution_convert_fusion.1 = bf16[1024,2048]{1,0:T(8,128)(2,1)} fusion(bf16[704,2048]{1,0:T(8,128)(2,1)} %all-gather.14.cloned.1.call-done, f32[1024,704]{0,1:T(8,128)} %fusion.114, bf16[1024,2048]{1,0:T(8,128)(2,1)} %all-gather.8.cloned.1.call-done, bf16[2048,704]{0,1:T(8,128)(2,1)} %all-gather.12.cloned.1.call-done), kind=kOutput, calls=%fused_computation.94 | convolution fusion | flops 5912002560 | bytes 17039360 | tf_op jit(solution)/shard_map/dot_general | solution.py:178
  409.5 21.5 %reduce-scatter.10.cloned.1.call-done = bf16[512,3]{1,0:T(8,128)(2,1)} async-done(((bf16[4096,3]{1,0:T(8,128)(2,1)}), bf16[512,3]{1,0:T(8,128)(2,1)}) %reduce-scatter.10.cloned.1.call-update) | async-done | bytes 3088
  431.0 1.6 copy.251
  432.6 31.0 %reduce-scatter.8.cloned.1.call-done = bf16[1,128,256]{2,1,0:T(8,128)(2,1)} async-done(((bf16[8,128,256]{2,1,0:T(8,128)(2,1)}), bf16[1,128,256]{2,1,0:T(8,128)(2,1)}) %reduce-scatter.8.cloned.1.call-update) | async-done | bytes 65552 | tf_op jit(solution)/shard_map/reduce_scatter | solution.py:144
  463.6 1.5 bitcast_convert_fusion
  465.1 37.8 %reduce-scatter.6.cloned.1.call-done = bf16[128,2048]{1,0:T(8,128)(2,1)} async-done(((bf16[1024,2048]{1,0:T(8,128)(2,1)}), bf16[128,2048]{1,0:T(8,128)(2,1)}) %reduce-scatter.6.cloned.1.call-update) | async-done | bytes 524304 | tf_op jit(solution)/shard_map/reduce_scatter | solution.py:177
  502.9 2.0 fusion.82
  (161 shorter events, 47.6 us)
Async XLA Ops:
  7.2 198.2 %copy-start = (f32[256]{0:T(256)S(1)}, f32[256]{0:T(256)}, u32[]{:S(2)}) copy-start(f32[256]{0:T(256)} %param.38) | copy-start | bytes 3076
  7.2 233.8 %all-gather.6.cloned.1.call-start = ((), (), s32[]{:S(2)}) async-start(), calls=%async_computation.3 | async-start | bytes 8454144 | tf_op jit(solution)/shard_map/all_gather | solution.py:160
  8.1 9.1 %collective-permute-start = (bf16[3,4096]{1,0:T(4,128)(2,1)S(1)}, bf16[3,4096]{1,0:T(4,128)(2,1)S(1)}, u32[]{:S(2)}, u32[]{:S(2)}) collective-permute-start(bf16[3,4096]{1,0:T(4,128)(2,1)S(1)} %slice_bitcast_fusion.2), channel_id=1, source_target_pairs={{0,1},{1,2},{2,3},{3,4},{4,5},{5,6},{6,7},{8,9},{9,10},{10,11},{11... | collective-permute-start | bytes 73736 | tf_op jit(solution)/shard_map/ppermute | solution.py:20
  9.4 249.4 %all-gather.10.cloned.1.call-start = ((), (), s32[]{:S(2)}) async-start(), calls=%async_computation.5 | async-start | bytes 3063808 | tf_op jit(solution)/shard_map/all_gather | solution.py:169
  20.6 1.7 copy-start.2
  23.9 83.9 %copy-start.9 = (f32[8,2,64,128]{3,0,2,1:T(8,128)}, f32[8,2,64,128]{3,0,2,1:T(8,128)S(1)}, u32[]{:S(2)}) copy-start(f32[8,2,64,128]{3,0,2,1:T(8,128)S(1)} %get-tuple-element.663) | copy-start | bytes 1572868
  23.9 85.7 %slice-start = ((f32[128,4096]{1,0:T(8,128)}), f32[128,2048]{1,0:T(8,128)S(1)}, s32[]{:S(2)}) async-start(f32[128,4096]{1,0:T(8,128)} %copy-done.2), calls=%async_computation.11 | async-start | bytes 2097152 | tf_op jit(solution)/shard_map/slice | solution.py:125
  116.8 6.6 %collective-permute-start.1 = (bf16[8,128,256]{2,1,0:T(8,128)(2,1)}, bf16[8,128,256]{2,1,0:T(8,128)(2,1)}, u32[]{:S(2)}, u32[]{:S(2)}) collective-permute-start(bf16[8,128,256]{2,1,0:T(8,128)(2,1)} %convert_element_type.129), channel_id=1, source_target_pairs={{0,1},{1,2},{2,3},{3,4},{4,5},{5,6},{6,7},{8,9},{9,10},{10,11},{11... | collective-permute-start | bytes 1572872 | tf_op jit(solution)/shard_map/ppermute | solution.py:20
  129.6 8.3 %collective-permute-start.2 = (bf16[8,128,256]{2,1,0:T(8,128)(2,1)}, bf16[8,128,256]{2,1,0:T(8,128)(2,1)}, u32[]{:S(2)}, u32[]{:S(2)}) collective-permute-start(bf16[8,128,256]{2,1,0:T(8,128)(2,1)} %convert_element_type.131), channel_id=1, source_target_pairs={{0,1},{1,2},{2,3},{3,4},{4,5},{5,6},{6,7},{8,9},{9,10},{10,11},{11... | collective-permute-start | bytes 1572872 | tf_op jit(solution)/shard_map/ppermute | solution.py:20
  144.2 10.8 %collective-permute-start.3 = (bf16[8,128,256]{2,1,0:T(8,128)(2,1)}, bf16[8,128,256]{2,1,0:T(8,128)(2,1)}, u32[]{:S(2)}, u32[]{:S(2)}) collective-permute-start(bf16[8,128,256]{2,1,0:T(8,128)(2,1)} %convert_element_type.133), channel_id=1, source_target_pairs={{0,1},{1,2},{2,3},{3,4},{4,5},{5,6},{6,7},{8,9},{9,10},{10,11},{11... | collective-permute-start | bytes 1572872 | tf_op jit(solution)/shard_map/ppermute | solution.py:20
  161.2 10.8 %collective-permute-start.4 = (bf16[8,128,256]{2,1,0:T(8,128)(2,1)}, bf16[8,128,256]{2,1,0:T(8,128)(2,1)}, u32[]{:S(2)}, u32[]{:S(2)}) collective-permute-start(bf16[8,128,256]{2,1,0:T(8,128)(2,1)} %convert_element_type.135), channel_id=1, source_target_pairs={{0,1},{1,2},{2,3},{3,4},{4,5},{5,6},{6,7},{8,9},{9,10},{10,11},{11... | collective-permute-start | bytes 1572872 | tf_op jit(solution)/shard_map/ppermute | solution.py:20
  178.3 10.8 %collective-permute-start.5 = (bf16[8,128,256]{2,1,0:T(8,128)(2,1)}, bf16[8,128,256]{2,1,0:T(8,128)(2,1)}, u32[]{:S(2)}, u32[]{:S(2)}) collective-permute-start(bf16[8,128,256]{2,1,0:T(8,128)(2,1)} %convert_element_type.137), channel_id=1, source_target_pairs={{0,1},{1,2},{2,3},{3,4},{4,5},{5,6},{6,7},{8,9},{9,10},{10,11},{11... | collective-permute-start | bytes 1572872 | tf_op jit(solution)/shard_map/ppermute | solution.py:20
  195.2 13.6 %collective-permute-start.6 = (bf16[8,128,256]{2,1,0:T(8,128)(2,1)}, bf16[8,128,256]{2,1,0:T(8,128)(2,1)}, u32[]{:S(2)}, u32[]{:S(2)}) collective-permute-start(bf16[8,128,256]{2,1,0:T(8,128)(2,1)} %convert_element_type.139), channel_id=1, source_target_pairs={{0,1},{1,2},{2,3},{3,4},{4,5},{5,6},{6,7},{8,9},{9,10},{10,11},{11... | collective-permute-start | bytes 1572872 | tf_op jit(solution)/shard_map/ppermute | solution.py:20
  205.0 87.8 %all-gather.8.cloned.1.call-start = ((), (), s32[]{:S(2)}) async-start(), calls=%async_computation.4 | async-start | bytes 4718592 | tf_op jit(solution)/shard_map/all_gather | solution.py:173
  214.2 7.6 %copy-start.4 = (f32[16,8,8,128]{3,2,1,0:T(8,128)S(1)}, f32[16,8,8,128]{3,2,1,0:T(8,128)}, u32[]{:S(2)}) copy-start(f32[16,8,8,128]{3,2,1,0:T(8,128)} %copy.258) | copy-start | bytes 1572868
  214.2 8.8 %copy-start.10 = (f32[8,2,64,128]{3,0,2,1:T(8,128)S(1)}, f32[8,2,64,128]{3,0,2,1:T(8,128)}, u32[]{:S(2)}) copy-start(f32[8,2,64,128]{3,0,2,1:T(8,128)} %copy-done.9) | copy-start | bytes 1572868
  214.2 10.6 %collective-permute-start.7 = (bf16[8,128,256]{2,1,0:T(8,128)(2,1)S(1)}, bf16[8,128,256]{2,1,0:T(8,128)(2,1)S(1)}, u32[]{:S(2)}, u32[]{:S(2)}) collective-permute-start(bf16[8,128,256]{2,1,0:T(8,128)(2,1)S(1)} %convert_element_type.141), channel_id=1, source_target_pairs={{0,1},{1,2},{2,3},{3,4},{4,5},{5,6},{6,7},{8,9},{9,10},{10,11},{11... | collective-permute-start | bytes 1572872 | tf_op jit(solution)/shard_map/ppermute | solution.py:20
  224.9 2.3 copy-start.3
  225.0 2.3 copy-start.6
  228.0 1.0 copy-start.7
  230.4 2.3 copy-start.3
  230.4 2.3 copy-start.6
  233.4 1.0 copy-start.7
  235.8 3.3 copy-start.8
  241.0 5.8 %copy-start.11 = (f32[2048]{0:T(1024)S(1)}, f32[2048]{0:T(1024)}, u32[]{:S(2)}) copy-start(f32[2048]{0:T(1024)} %param.40) | copy-start | bytes 24580
  241.0 8.6 %copy-start.5 = (bf16[1,128,4096]{2,1,0:T(8,128)(2,1)S(1)}, bf16[1,128,4096]{2,1,0:T(8,128)(2,1)}, u32[]{:S(2)}) copy-start(bf16[1,128,4096]{2,1,0:T(8,128)(2,1)} %param.30) | copy-start | bytes 3145732
  247.8 97.3 %all-gather.12.cloned.1.call-start = ((), (), s32[]{:S(2)}) async-start(), calls=%async_computation.6 | async-start | bytes 3063808 | tf_op jit(solution)/shard_map/all_gather | solution.py:170
  248.4 148.5 %all-gather.14.cloned.1.call-start = ((), (), s32[]{:S(2)}) async-start(), calls=%async_computation.7 | async-start | bytes 3063808 | tf_op jit(solution)/shard_map/all_gather | solution.py:172
  249.0 182.0 %reduce-scatter.10.cloned.1.call-start = ((), (), s32[]{:S(2)}) async-start(), calls=%async_computation.10 | async-start | bytes 1179648
  251.3 212.2 %reduce-scatter.8.cloned.1.call-start = ((), (), s32[]{:S(2)}) async-start(), calls=%async_computation.9 | async-start | bytes 589824 | tf_op jit(solution)/shard_map/reduce_scatter | solution.py:144
  252.3 250.5 %reduce-scatter.6.cloned.1.call-start = ((), (), s32[]{:S(2)}) async-start(), calls=%async_computation.8 | async-start | bytes 4718592 | tf_op jit(solution)/shard_map/reduce_scatter | solution.py:177
  408.9 96.0 %copy-start.1 = (f32[256]{0:T(256)S(1)}, f32[256]{0:T(256)}, u32[]{:S(2)}) copy-start(f32[256]{0:T(256)} %param.38) | copy-start | bytes 3076
Sparse Core Ops, SparseCore 0:
  11.0 74.0 all-gather.5
  205.1 53.6 all-gather.9
  261.1 31.6 all-gather.7
  294.8 50.2 all-gather.11
  347.0 49.8 all-gather.13
  399.2 31.8 reduce-scatter.9
  433.4 30.1 reduce-scatter.7
  466.0 36.8 reduce-scatter.5
where the time goes:
time: 521 us; the launch traced here: 512 us
  waiting for transfers between devices  233 us (45%)
  other arithmetic  114 us (22%)
  matrix products  71.7 us (14%)
  starting transfers between devices  60.5 us (12%)
  local copies, waits for them, and re-layouts  16.5 us (3%)
  between operations  15.4 us (3%)
    another operation x4, other arithmetic, block_tables(): lax.linalg.triangular_solve(identity + couple, identity, left_side=True,...  80.1 us
    ppermute x8, starting transfers between devices, shifted(): lax.ppermute(value, axis, [(source, source + steps) for source in range(i...  59.8 us
    all_gather x1, waiting for transfers between devices, local(): down_full = lax.all_gather(w_down, 'req', axis=1, tiled=True)  51.8 us
    all_gather x1, waiting for transfers between devices, local(): lax.all_gather(w_up, 'req', axis=0, tiled=True)  44.4 us
    reduce_scatter x1, waiting for transfers between devices, local(): lax.psum_scatter(jnp.dot(inner_units, down_full, preferred_element_type=j...  37.8 us
    all_gather x1, waiting for transfers between devices, local(): shard_rows = lax.all_gather(normed, 'seq', axis=0, tiled=True)  34 us
    reduce_scatter x1, waiting for transfers between devices, local(): lax.psum_scatter(state_term.astype(jnp.bfloat16), 'seq', scatter_dimensio...  31 us
    unnamed x9, waiting for transfers between devices  22.7 us
  transfers between devices with their start and end apart: 16, of which 12 were waited for; matrix products, arithmetic and copies ran while one was open for 39% of the time, Pallas kernels for 0%

commit v1 on v0

--- a/solution.py
+++ b/solution.py
@@ -169,7 +169,9 @@
         lax.all_gather(w_gate, "req", axis=0, tiled=True),
         lax.all_gather(w_up, "req", axis=0, tiled=True),
     )
-    down_full = lax.all_gather(w_down, "req", axis=1, tiled=True)
+    down_full = jnp.concatenate(
+        lax.all_to_all(jnp.stack([w_down] * lax.axis_size("req")), "req", 0, 0), axis=1
+    )
     shard_rows = lax.all_gather(normed, "seq", axis=0, tiled=True)
     gate_part = jnp.dot(shard_rows, gate_full, preferred_element_type=jnp.float32)
     upward = jnp.dot(shard_rows, up_full, preferred_element_type=jnp.float32)

time: 521 us -> 478 us (0.917)
  waiting for transfers between devices: 233 us -> 179 us
  starting transfers between devices: 60.5 us -> 67.6 us
    all_gather x1 -> x0, waiting for transfers between devices: 51.8 us -> none  [local(): down_full = lax.all_gather(w_down, 'req', axis=1, tiled=True)]
    all_to_all x0 -> x1, starting transfers between devices: none -> 7.19 us  [local(): lax.all_to_all(jnp.stack([w_down] * lax.axis_size('req')), 'req', 0, 0)]
    all_gather x1, waiting for transfers between devices: 6.25 us -> 0.02 us  [local(): lax.all_gather(w_gate, 'req', axis=0, tiled=True)]
    unnamed x32 -> x40, local copies, waits for them, and re-layouts: 9.73 us -> 10.5 us
    unnamed x9 -> x8, waiting for transfers between devices: 22.7 us -> 22 us
  transfers between devices with their start and end apart: 16 -> 16, of which waited for: 12 -> 10; matrix products, arithmetic and copies ran while one was open for 39% -> 43% of each run, Pallas kernels for 0% -> 0%
where the time goes in v1:
time: 478 us; the launch traced here: 470 us
  waiting for transfers between devices  179 us (37%)
  other arithmetic  116 us (24%)
  matrix products  71.6 us (15%)
  starting transfers between devices  67.6 us (14%)
  local copies, waits for them, and re-layouts  19.4 us (4%)
  between operations  15.6 us (3%)
    another operation x4, other arithmetic, block_tables(): lax.linalg.triangular_solve(identity + couple, identity, left_side=True,...  80.7 us
    ppermute x8, starting transfers between devices, shifted(): lax.ppermute(value, axis, [(source, source + steps) for source in range(i...  59.7 us
    all_gather x1, waiting for transfers between devices, local(): lax.all_gather(w_up, 'req', axis=0, tiled=True)  44.4 us
    all_gather x1, waiting for transfers between devices, local(): shard_rows = lax.all_gather(normed, 'seq', axis=0, tiled=True)  38.7 us
    reduce_scatter x1, waiting for transfers between devices, local(): lax.psum_scatter(jnp.dot(inner_units, down_full, preferred_element_type=j...  37.8 us
    reduce_scatter x1, waiting for transfers between devices, local(): lax.psum_scatter(state_term.astype(jnp.bfloat16), 'seq', scatter_dimensio...  30.8 us
    unnamed x8, waiting for transfers between devices  22 us
    dot_general x16, matrix products, advance(): jnp.einsum('hck,hcx->hkx', keys_now, corrected, precision=HIGHEST)  21.1 us
  transfers between devices with their start and end apart: 16, of which 10 were waited for; matrix products, arithmetic and copies ran while one was open for 43% of the time, Pallas kernels for 0%

profile of v1, /device:TPU:0, one launch (start us, length us, event | category | flops | bytes accessed | tf_op | source)
XLA Modules:
  0.0 469.5 jit_solution(6112004581645283876)
XLA Ops:
  8.1 1.3 collective-permute-start
  11.0 1.3 fusion.107
  12.3 2.0 fusion.108
  17.9 3.4 divide_multiply_fusion
  21.3 1.4 multiply_bitcast_fusion
  23.6 1.3 reduce_sum.56
  25.1 1.1 copy.259
  27.4 1.8 fusion.74
  29.2 80.0 %custom-call.3 = f32[8,2,1,64,64]{3,4,2,1,0:T(8,128)} custom-call(f32[8,2,1,64,64]{4,3,2,1,0:T(8,128)} %fusion.74), custom_call_target="InvertDiagBlocksLowerTriangular" | custom-call | tf_op jit(solution)/shard_map/triangular_solve | solution.py:45
  109.2 2.0 fusion.87
  111.2 1.7 convolution_bitcast_fusion.2
  113.4 1.3 convolution_bitcast_fusion
  115.3 4.1 while.90
  116.0 1.3 convolution_add_fusion.25
  118.1 1.3 convolution_add_fusion.25
  120.3 5.9 %collective-permute-start.1 = (bf16[8,128,256]{2,1,0:T(8,128)(2,1)}, bf16[8,128,256]{2,1,0:T(8,128)(2,1)}, u32[]{:S(2)}, u32[]{:S(2)}) collective-permute-start(bf16[8,128,256]{2,1,0:T(8,128)(2,1)} %convert_element_type.129), channel_id=1, source_target_pairs={{0,1},{1,2},{2,3},{3,4},{4,5},{5,6},{6,7},{8,9},{9,10},{10,11},{11... | collective-permute-start | bytes 1572872 | tf_op jit(solution)/shard_map/ppermute | solution.py:20
  128.0 4.2 while.83
  128.7 1.3 convolution_add_fusion.18
  130.8 1.3 convolution_add_fusion.18
  133.1 7.3 %collective-permute-start.2 = (bf16[8,128,256]{2,1,0:T(8,128)(2,1)}, bf16[8,128,256]{2,1,0:T(8,128)(2,1)}, u32[]{:S(2)}, u32[]{:S(2)}) collective-permute-start(bf16[8,128,256]{2,1,0:T(8,128)(2,1)} %convert_element_type.131), channel_id=1, source_target_pairs={{0,1},{1,2},{2,3},{3,4},{4,5},{5,6},{6,7},{8,9},{9,10},{10,11},{11... | collective-permute-start | bytes 1572872 | tf_op jit(solution)/shard_map/ppermute | solution.py:20
  142.6 4.2 while.84
  143.3 1.3 convolution_add_fusion.19
  145.4 1.3 convolution_add_fusion.19
  147.7 9.7 %collective-permute-start.3 = (bf16[8,128,256]{2,1,0:T(8,128)(2,1)}, bf16[8,128,256]{2,1,0:T(8,128)(2,1)}, u32[]{:S(2)}, u32[]{:S(2)}) collective-permute-start(bf16[8,128,256]{2,1,0:T(8,128)(2,1)} %convert_element_type.133), channel_id=1, source_target_pairs={{0,1},{1,2},{2,3},{3,4},{4,5},{5,6},{6,7},{8,9},{9,10},{10,11},{11... | collective-permute-start | bytes 1572872 | tf_op jit(solution)/shard_map/ppermute | solution.py:20
  159.6 4.2 while.85
  160.4 1.3 convolution_add_fusion.20
  162.5 1.3 convolution_add_fusion.20
  164.7 9.7 %collective-permute-start.4 = (bf16[8,128,256]{2,1,0:T(8,128)(2,1)}, bf16[8,128,256]{2,1,0:T(8,128)(2,1)}, u32[]{:S(2)}, u32[]{:S(2)}) collective-permute-start(bf16[8,128,256]{2,1,0:T(8,128)(2,1)} %convert_element_type.135), channel_id=1, source_target_pairs={{0,1},{1,2},{2,3},{3,4},{4,5},{5,6},{6,7},{8,9},{9,10},{10,11},{11... | collective-permute-start | bytes 1572872 | tf_op jit(solution)/shard_map/ppermute | solution.py:20
  176.7 4.2 while.86
  177.4 1.3 convolution_add_fusion.21
  179.5 1.3 convolution_add_fusion.21
  181.8 9.7 %collective-permute-start.5 = (bf16[8,128,256]{2,1,0:T(8,128)(2,1)}, bf16[8,128,256]{2,1,0:T(8,128)(2,1)}, u32[]{:S(2)}, u32[]{:S(2)}) collective-permute-start(bf16[8,128,256]{2,1,0:T(8,128)(2,1)} %convert_element_type.137), channel_id=1, source_target_pairs={{0,1},{1,2},{2,3},{3,4},{4,5},{5,6},{6,7},{8,9},{9,10},{10,11},{11... | collective-permute-start | bytes 1572872 | tf_op jit(solution)/shard_map/ppermute | solution.py:20
  193.7 4.2 while.87
  194.5 1.3 convolution_add_fusion.22
  196.6 1.3 convolution_add_fusion.22
  198.8 9.7 %collective-permute-start.6 = (bf16[8,128,256]{2,1,0:T(8,128)(2,1)}, bf16[8,128,256]{2,1,0:T(8,128)(2,1)}, u32[]{:S(2)}, u32[]{:S(2)}) collective-permute-start(bf16[8,128,256]{2,1,0:T(8,128)(2,1)} %convert_element_type.139), channel_id=1, source_target_pairs={{0,1},{1,2},{2,3},{3,4},{4,5},{5,6},{6,7},{8,9},{9,10},{10,11},{11... | collective-permute-start | bytes 1572872 | tf_op jit(solution)/shard_map/ppermute | solution.py:20
  210.5 1.9 copy.262
  213.5 4.2 while.88
  214.3 1.3 convolution_add_fusion.23
  216.4 1.3 convolution_add_fusion.23
  217.8 6.3 %collective-permute-start.7 = (bf16[8,128,256]{2,1,0:T(8,128)(2,1)S(1)}, bf16[8,128,256]{2,1,0:T(8,128)(2,1)S(1)}, u32[]{:S(2)}, u32[]{:S(2)}) collective-permute-start(bf16[8,128,256]{2,1,0:T(8,128)(2,1)S(1)} %convert_element_type.141), channel_id=1, source_target_pairs={{0,1},{1,2},{2,3},{3,4},{4,5},{5,6},{6,7},{8,9},{9,10},{10,11},{11... | collective-permute-start | bytes 1572872 | tf_op jit(solution)/shard_map/ppermute | solution.py:20
  224.1 1.2 fusion.97
  226.5 1.9 fusion.72
  228.5 10.9 %while.89 = (s32[]{:T(128)}, f32[8,128,256]{2,1,0:T(8,128)S(1)}, f32[2,8,64,256]{3,2,1,0:T(8,128)}, f32[2,8]{1,0:T(2,128)S(1)}, f32[2,8,64,128]{3,2,1,0:T(8,128)...) while((s32[]{:T(128)}, f32[8,128,256]{2,1,0:T(8,128)S(1)}, ...), condition=%wide.region_20.21_spmd, body=%wide.region_19.20_spmd.sunk | while | flops 705429504 | bytes 19925256 | solution.py:85
  229.3 1.5 fusion.225
  232.6 1.3 convolution_add_fusion.24
  234.7 1.5 fusion.225
  238.0 1.3 convolution_add_fusion.24
  239.4 1.5 multiply_reduce_fusion.1
  241.2 1.4 copy.265
  243.6 5.5 %multiply_reduce_fusion = (f32[128]{0:T(128)S(1)}, f32[128,2048]{1,0:T(8,128)S(1)}) fusion(bf16[2048,2048]{1,0:T(8,128)(2,1)} %all-gather.5.cloned.1.call-done, f32[128,2048]{1,0:T(8,128)S(1)} %bitcast.355, f32[128,2048]{1,0:T(8,128)} %bitcast.354, bf16[1,128,2048]{2,1,0:T(8,128)(2,1)} %param.31, f32[2048]{0:T(1024)S(1)} %bitcast.367, ...), kind=kOutput, calls=%fused_computation.127 | convolution fusion | flops 1077673856 | bytes 12591616 | tf_op jit(solution)/shard_map/dot_general | solution.py:158
  250.7 2.2 stack.2
  252.9 7.2 %all-to-all-start = ((bf16[16,704,128]{2,1,0:T(8,128)(2,1)}), bf16[16,704,128]{2,1,0:T(8,128)(2,1)}, u32[]{:S(2)}, u32[]{:S(2)}) async-start(bf16[16,704,128]{2,1,0:T(8,128)(2,1)} %stack.2), calls=%async_computation | async-start | bytes 5767168 | tf_op jit(solution)/shard_map/all_to_all | solution.py:173
  261.3 1.4 copy.253
  263.8 38.7 %all-gather.7.cloned.1.call-done = bf16[1024,2048]{1,0:T(8,128)(2,1)} async-done(((bf16[128,2048]{1,0:T(8,128)(2,1)}), bf16[1024,2048]{1,0:T(8,128)(2,1)}) %all-gather.7.cloned.1.call-update) | async-done | bytes 4194320 | tf_op jit(solution)/shard_map/all_gather | solution.py:175
  302.4 7.8 %fusion.116 = f32[1024,704]{0,1:T(8,128)} fusion(bf16[1024,2048]{1,0:T(8,128)(2,1)} %all-gather.7.cloned.1.call-done, bf16[2048,704]{0,1:T(8,128)(2,1)} %all-gather.9.cloned.1.call-done), kind=kOutput, calls=%fused_computation.197 | convolution fusion | flops 2952790016 | bytes 9961472 | tf_op jit(solution)/shard_map/dot_general | solution.py:176
  310.3 44.4 %all-gather.11.cloned.1.call-done = bf16[2048,704]{0,1:T(8,128)(2,1)} async-done(((bf16[128,704]{0,1:T(8,128)(2,1)}), bf16[2048,704]{0,1:T(8,128)(2,1)}) %all-gather.11.cloned.1.call-update) | async-done | bytes 2883600 | tf_op jit(solution)/shard_map/all_gather | solution.py:170
  354.7 12.0 %convolution_convert_fusion.1 = bf16[1024,2048]{1,0:T(8,128)(2,1)} fusion(f32[1024,704]{0,1:T(8,128)} %fusion.116, bf16[1024,2048]{1,0:T(8,128)(2,1)} %all-gather.7.cloned.1.call-done, bf16[2048,704]{0,1:T(8,128)(2,1)} %all-gather.11.cloned.1.call-done, bf16[16,704,128]{2,1,0:T(8,128)(2,1)} %all-to-all-done), kind=kOutput, calls=%fused_computation.94 | convolution fusion | flops 5912002560 | bytes 17039360 | tf_op jit(solution)/shard_map/dot_general | solution.py:180
  367.4 21.4 %reduce-scatter.10.cloned.1.call-done = bf16[512,3]{1,0:T(8,128)(2,1)} async-done(((bf16[4096,3]{1,0:T(8,128)(2,1)}), bf16[512,3]{1,0:T(8,128)(2,1)}) %reduce-scatter.10.cloned.1.call-update) | async-done | bytes 3088
  388.8 1.6 copy.254
  390.4 30.8 %reduce-scatter.8.cloned.1.call-done = bf16[1,128,256]{2,1,0:T(8,128)(2,1)} async-done(((bf16[8,128,256]{2,1,0:T(8,128)(2,1)}), bf16[1,128,256]{2,1,0:T(8,128)(2,1)}) %reduce-scatter.8.cloned.1.call-update) | async-done | bytes 65552 | tf_op jit(solution)/shard_map/reduce_scatter | solution.py:144
  421.2 1.5 bitcast_convert_fusion
  422.7 37.8 %reduce-scatter.6.cloned.1.call-done = bf16[128,2048]{1,0:T(8,128)(2,1)} async-done(((bf16[1024,2048]{1,0:T(8,128)(2,1)}), bf16[128,2048]{1,0:T(8,128)(2,1)}) %reduce-scatter.6.cloned.1.call-update) | async-done | bytes 524304 | tf_op jit(solution)/shard_map/reduce_scatter | solution.py:179
  460.5 2.0 fusion.84
  (169 shorter events, 49.8 us)
Async XLA Ops:
  7.2 201.7 %copy-start = (f32[256]{0:T(256)S(1)}, f32[256]{0:T(256)}, u32[]{:S(2)}) copy-start(f32[256]{0:T(256)} %param.38) | copy-start | bytes 3076
  7.2 236.4 %all-gather.5.cloned.1.call-start = ((), (), s32[]{:S(2)}) async-start(), calls=%async_computation.4 | async-start | bytes 8454144 | tf_op jit(solution)/shard_map/all_gather | solution.py:160
  8.1 9.8 %collective-permute-start = (bf16[3,4096]{1,0:T(4,128)(2,1)S(1)}, bf16[3,4096]{1,0:T(4,128)(2,1)S(1)}, u32[]{:S(2)}, u32[]{:S(2)}) collective-permute-start(bf16[3,4096]{1,0:T(4,128)(2,1)S(1)} %slice_bitcast_fusion.2), channel_id=1, source_target_pairs={{0,1},{1,2},{2,3},{3,4},{4,5},{5,6},{6,7},{8,9},{9,10},{10,11},{11... | collective-permute-start | bytes 73736 | tf_op jit(solution)/shard_map/ppermute | solution.py:20
  9.4 254.4 %all-gather.9.cloned.1.call-start = ((), (), s32[]{:S(2)}) async-start(), calls=%async_computation.6 | async-start | bytes 3063808 | tf_op jit(solution)/shard_map/all_gather | solution.py:169
  21.3 2.3 copy-start.2
  22.7 4.6 copy-start.15
  26.2 85.0 %copy-start.5 = (f32[16,8,8,128]{3,2,1,0:T(8,128)}, f32[16,8,8,128]{3,2,1,0:T(8,128)S(1)}, u32[]{:S(2)}) copy-start(f32[16,8,8,128]{3,2,1,0:T(8,128)S(1)} %copy.259) | copy-start | bytes 1572868
  27.4 1.8 copy-start.11
  27.4 85.7 %slice-start = ((f32[128,4096]{1,0:T(8,128)}), f32[128,2048]{1,0:T(8,128)S(1)}, s32[]{:S(2)}) async-start(f32[128,4096]{1,0:T(8,128)} %copy-done.2), calls=%async_computation.11 | async-start | bytes 2097152 | tf_op jit(solution)/shard_map/slice | solution.py:125
  113.4 1.4 copy-start.6
  120.3 6.5 %collective-permute-start.1 = (bf16[8,128,256]{2,1,0:T(8,128)(2,1)}, bf16[8,128,256]{2,1,0:T(8,128)(2,1)}, u32[]{:S(2)}, u32[]{:S(2)}) collective-permute-start(bf16[8,128,256]{2,1,0:T(8,128)(2,1)} %convert_element_type.129), channel_id=1, source_target_pairs={{0,1},{1,2},{2,3},{3,4},{4,5},{5,6},{6,7},{8,9},{9,10},{10,11},{11... | collective-permute-start | bytes 1572872 | tf_op jit(solution)/shard_map/ppermute | solution.py:20
  133.1 8.3 %collective-permute-start.2 = (bf16[8,128,256]{2,1,0:T(8,128)(2,1)}, bf16[8,128,256]{2,1,0:T(8,128)(2,1)}, u32[]{:S(2)}, u32[]{:S(2)}) collective-permute-start(bf16[8,128,256]{2,1,0:T(8,128)(2,1)} %convert_element_type.131), channel_id=1, source_target_pairs={{0,1},{1,2},{2,3},{3,4},{4,5},{5,6},{6,7},{8,9},{9,10},{10,11},{11... | collective-permute-start | bytes 1572872 | tf_op jit(solution)/shard_map/ppermute | solution.py:20
  147.7 10.8 %collective-permute-start.3 = (bf16[8,128,256]{2,1,0:T(8,128)(2,1)}, bf16[8,128,256]{2,1,0:T(8,128)(2,1)}, u32[]{:S(2)}, u32[]{:S(2)}) collective-permute-start(bf16[8,128,256]{2,1,0:T(8,128)(2,1)} %convert_element_type.133), channel_id=1, source_target_pairs={{0,1},{1,2},{2,3},{3,4},{4,5},{5,6},{6,7},{8,9},{9,10},{10,11},{11... | collective-permute-start | bytes 1572872 | tf_op jit(solution)/shard_map/ppermute | solution.py:20
  164.7 10.8 %collective-permute-start.4 = (bf16[8,128,256]{2,1,0:T(8,128)(2,1)}, bf16[8,128,256]{2,1,0:T(8,128)(2,1)}, u32[]{:S(2)}, u32[]{:S(2)}) collective-permute-start(bf16[8,128,256]{2,1,0:T(8,128)(2,1)} %convert_element_type.135), channel_id=1, source_target_pairs={{0,1},{1,2},{2,3},{3,4},{4,5},{5,6},{6,7},{8,9},{9,10},{10,11},{11... | collective-permute-start | bytes 1572872 | tf_op jit(solution)/shard_map/ppermute | solution.py:20
  181.8 10.8 %collective-permute-start.5 = (bf16[8,128,256]{2,1,0:T(8,128)(2,1)}, bf16[8,128,256]{2,1,0:T(8,128)(2,1)}, u32[]{:S(2)}, u32[]{:S(2)}) collective-permute-start(bf16[8,128,256]{2,1,0:T(8,128)(2,1)} %convert_element_type.137), channel_id=1, source_target_pairs={{0,1},{1,2},{2,3},{3,4},{4,5},{5,6},{6,7},{8,9},{9,10},{10,11},{11... | collective-permute-start | bytes 1572872 | tf_op jit(solution)/shard_map/ppermute | solution.py:20
  198.8 13.6 %collective-permute-start.6 = (bf16[8,128,256]{2,1,0:T(8,128)(2,1)}, bf16[8,128,256]{2,1,0:T(8,128)(2,1)}, u32[]{:S(2)}, u32[]{:S(2)}) collective-permute-start(bf16[8,128,256]{2,1,0:T(8,128)(2,1)} %convert_element_type.139), channel_id=1, source_target_pairs={{0,1},{1,2},{2,3},{3,4},{4,5},{5,6},{6,7},{8,9},{9,10},{10,11},{11... | collective-permute-start | bytes 1572872 | tf_op jit(solution)/shard_map/ppermute | solution.py:20
  208.5 93.9 %all-gather.7.cloned.1.call-start = ((), (), s32[]{:S(2)}) async-start(), calls=%async_computation.5 | async-start | bytes 4718592 | tf_op jit(solution)/shard_map/all_gather | solution.py:175
  217.7 7.7 %copy-start.4 = (f32[16,8,8,128]{3,2,1,0:T(8,128)S(1)}, f32[16,8,8,128]{3,2,1,0:T(8,128)}, u32[]{:S(2)}) copy-start(f32[16,8,8,128]{3,2,1,0:T(8,128)} %copy.262) | copy-start | bytes 1572868
  217.7 8.8 %copy-start.12 = (f32[8,2,64,128]{3,0,2,1:T(8,128)S(1)}, f32[8,2,64,128]{3,0,2,1:T(8,128)}, u32[]{:S(2)}) copy-start(f32[8,2,64,128]{3,0,2,1:T(8,128)} %copy-done.11) | copy-start | bytes 1572868
  217.8 10.6 %collective-permute-start.7 = (bf16[8,128,256]{2,1,0:T(8,128)(2,1)S(1)}, bf16[8,128,256]{2,1,0:T(8,128)(2,1)S(1)}, u32[]{:S(2)}, u32[]{:S(2)}) collective-permute-start(bf16[8,128,256]{2,1,0:T(8,128)(2,1)S(1)} %convert_element_type.141), channel_id=1, source_target_pairs={{0,1},{1,2},{2,3},{3,4},{4,5},{5,6},{6,7},{8,9},{9,10},{10,11},{11... | collective-permute-start | bytes 1572872 | tf_op jit(solution)/shard_map/ppermute | solution.py:20
  228.5 2.3 copy-start.3
  228.5 2.3 copy-start.8
  231.6 1.0 copy-start.9
  233.9 2.3 copy-start.3
  233.9 2.3 copy-start.8
  237.0 1.0 copy-start.9
  239.4 3.2 copy-start.10
  243.6 5.5 %copy-start.14 = (f32[2048]{0:T(1024)S(1)}, f32[2048]{0:T(1024)}, u32[]{:S(2)}) copy-start(f32[2048]{0:T(1024)} %param.40) | copy-start | bytes 24580
  243.6 7.1 %copy-start.13 = (bf16[704,128]{1,0:T(8,128)(2,1)S(1)}, bf16[704,128]{1,0:T(8,128)(2,1)}, u32[]{:S(2)}) copy-start(bf16[704,128]{1,0:T(8,128)(2,1)} %param.43) | copy-start | bytes 540676
  250.1 104.6 %all-gather.11.cloned.1.call-start = ((), (), s32[]{:S(2)}) async-start(), calls=%async_computation.7 | async-start | bytes 3063808 | tf_op jit(solution)/shard_map/all_gather | solution.py:170
  252.9 8.1 %copy-start.7 = (bf16[1,128,4096]{2,1,0:T(8,128)(2,1)S(1)}, bf16[1,128,4096]{2,1,0:T(8,128)(2,1)}, u32[]{:S(2)}) copy-start(bf16[1,128,4096]{2,1,0:T(8,128)(2,1)} %param.30) | copy-start | bytes 3145732
  252.9 57.4 %all-to-all-start = ((bf16[16,704,128]{2,1,0:T(8,128)(2,1)}), bf16[16,704,128]{2,1,0:T(8,128)(2,1)}, u32[]{:S(2)}, u32[]{:S(2)}) async-start(bf16[16,704,128]{2,1,0:T(8,128)(2,1)} %stack.2), calls=%async_computation | async-start | bytes 5767168 | tf_op jit(solution)/shard_map/all_to_all | solution.py:173
  260.1 128.7 %reduce-scatter.10.cloned.1.call-start = ((), (), s32[]{:S(2)}) async-start(), calls=%async_computation.10 | async-start | bytes 1179648
  262.7 158.5 %reduce-scatter.8.cloned.1.call-start = ((), (), s32[]{:S(2)}) async-start(), calls=%async_computation.9 | async-start | bytes 589824 | tf_op jit(solution)/shard_map/reduce_scatter | solution.py:144
  263.7 196.8 %reduce-scatter.6.cloned.1.call-start = ((), (), s32[]{:S(2)}) async-start(), calls=%async_computation.8 | async-start | bytes 4718592 | tf_op jit(solution)/shard_map/reduce_scatter | solution.py:179
  366.7 95.8 %copy-start.1 = (f32[256]{0:T(256)S(1)}, f32[256]{0:T(256)}, u32[]{:S(2)}) copy-start(f32[256]{0:T(256)} %param.38) | copy-start | bytes 3076
Sparse Core Ops, SparseCore 0:
  11.0 73.5 all-gather.4
  208.7 53.6 all-gather.8
  264.7 37.7 all-gather.6
  304.4 50.2 all-gather.10
  356.9 31.7 reduce-scatter.9
  391.0 30.1 reduce-scatter.7
  423.6 36.8 reduce-scatter.5
